TPU v7x, 1024 devices: a whole 4x8x16 slice. The times are simulated.
1024 devices in a mesh: ctx: 64 (over z, x), head: 16 (over y, core).
Axes of the slice: x: 4, y: 8, z: 16, core: 2. Of those that a mesh axis runs over, the one named last changes fastest.
Arguments:
- query: bfloat16 [16384, 6144], P('ctx', 'head'), may hold values from -6 to 6
- key_in: bfloat16 [16384, 6144], P('ctx', 'head'), may hold values from -6 to 6
- value: bfloat16 [16384, 6144], P('ctx', 'head'), may hold values from -6 to 6
- out_weight: bfloat16 [6144, 6144], P('head'), may hold values from -0.078125 to 0.078125
- grad_layer: bfloat16 [16384, 6144], P(('ctx', 'head')), may hold values from -6 to 6
- decay_exp: int32 [48], P('head'), may hold values from 5 to 22
Outputs:
- grad_query: bfloat16 [16384, 6144], P('ctx', 'head')
- grad_key: bfloat16 [16384, 6144], P('ctx', 'head')
- grad_value: bfloat16 [16384, 6144], P('ctx', 'head')
All inputs are finite; a program needn't handle non-finite values.
Results may differ from a plain program's by a relative error of at most 0.013.
Values may be sent and summed in bfloat16 or wider, within the bound.
A program may use at most 64 MiB of HBM per device.

v0:
```python
import jax
import jax.numpy as jnp
from jax import lax
from jax.sharding import PartitionSpec as P

BLOCK = 256


EPSILON = 1e-06


def prefix(part, axis, combine, identity, reverse):
    count = lax.axis_size(axis)
    place = lax.axis_index(axis)
    ahead = count - 1 - place if reverse else place
    gathered = jax.tree.map(lambda a: lax.all_gather(a, axis), part)
    state = jax.tree.map(lambda a, e: jnp.zeros_like(a) + jnp.asarray(e, a.dtype), part, identity)

    def one(turn, state):
        source = count - 1 - turn if reverse else turn
        return combine(
            state, jax.tree.map(lambda a: lax.dynamic_index_in_dim(a, source, 0, False), gathered)
        )

    return lax.fori_loop(0, ahead, one, state)


def combine(earlier, later):
    return (earlier[0] * later[0], later[0][:, None, None] * earlier[1] + later[1])


def body(query, key_in, value, out_weight, grad_layer, decay_exp):
    row_count = query.shape[0]
    head_count = decay_exp.shape[0]
    head_width = query.shape[1] // head_count
    block_count = row_count // BLOCK
    highest = lax.Precision.HIGHEST
    layer_whole = lax.all_gather(grad_layer, "head", axis=0, tiled=True)
    dnormed = lax.dot_general(
        layer_whole, out_weight, (((1,), (1,)), ((), ())), preferred_element_type=jnp.float32
    ).astype(jnp.bfloat16)
    queries = query.reshape(row_count, head_count, head_width)
    keys_in = key_in.reshape(row_count, head_count, head_width)
    values_in = value.reshape(row_count, head_count, head_width)
    cotangent = dnormed.reshape(row_count, head_count, head_width)
    log_rate = jnp.log1p(-jnp.exp2(-decay_exp.astype(jnp.float32)))
    offsets = jnp.arange(BLOCK).astype(jnp.float32)
    spread = offsets[:, None] - offsets[None, :]
    decay_mask = jnp.where(
        spread[None] >= 0, jnp.exp(jnp.maximum(spread, 0.0)[None] * log_rate[:, None, None]), 0.0
    )
    query_decay = jnp.exp((offsets + 1.0)[:, None] * log_rate[None, :])[:, :, None]
    key_decay = jnp.exp((BLOCK - 1.0 - offsets)[:, None] * log_rate[None, :])[:, :, None]
    block_decay = jnp.exp(BLOCK * log_rate)[:, None, None]
    device_decay = jnp.exp(row_count * log_rate)
    empty = jnp.zeros((head_count, head_width, head_width), jnp.float32)
    local_state = empty
    term = jnp.einsum(
        "jhd,jhe->hde",
        keys_in.astype(jnp.float32) * key_decay,
        values_in.astype(jnp.float32),
        precision=highest,
    )
    local_state = block_decay * local_state + term
    _, state = prefix(
        (device_decay, local_state),
        "ctx",
        combine,
        (jnp.ones((head_count,), jnp.float32), empty),
        False,
    )
    query_block = queries
    scores = jnp.einsum("ihd,jhd->hij", query_block, keys_in, preferred_element_type=jnp.float32)
    weights = (scores * decay_mask).astype(jnp.bfloat16)
    output = jnp.einsum("hij,jhe->ihe", weights, values_in, preferred_element_type=jnp.float32)
    output = output + jnp.einsum(
        "ihd,hde->ihe", query_block.astype(jnp.float32) * query_decay, state, precision=highest
    )
    block_states = [state]
    square_mean = jnp.mean(output * output, axis=-1, keepdims=True) + EPSILON
    inverse = lax.rsqrt(square_mean)
    normed = output * inverse
    cot_float = cotangent.astype(jnp.float32)
    dout = (
        (cot_float - normed * jnp.mean(cot_float * normed, axis=-1, keepdims=True)) * inverse
    ).astype(jnp.bfloat16)
    number = 0
    query_terms = [
        jnp.einsum(
            "ihd,ihe->hde",
            queries.astype(jnp.float32) * query_decay,
            dout.astype(jnp.float32),
            precision=highest,
        )
    ]
    local_back = empty
    for number in reversed(range(block_count)):
        local_back = block_decay * local_back + query_terms[number]
    _, back = prefix(
        (device_decay, local_back),
        "ctx",
        combine,
        (jnp.ones((head_count,), jnp.float32), empty),
        True,
    )
    grad_q_parts = []
    grad_k_parts = []
    grad_v_parts = []
    for number in reversed(range(block_count)):
        query_block = queries
        scores = jnp.einsum(
            "ihd,jhd->hij", query_block, keys_in, preferred_element_type=jnp.float32
        )
        weights = (scores * decay_mask).astype(jnp.bfloat16)
        dscores = jnp.einsum("ihe,jhe->hij", dout, values_in, preferred_element_type=jnp.float32)
        dweights = (dscores * decay_mask).astype(jnp.bfloat16)
        grad_q = jnp.einsum("hij,jhd->ihd", dweights, keys_in, preferred_element_type=jnp.float32)
        grad_q = grad_q + jnp.einsum(
            "ihe,hde->ihd",
            dout.astype(jnp.float32) * query_decay,
            block_states[number],
            precision=highest,
        )
        grad_k = jnp.einsum(
            "hij,ihd->jhd", dweights, query_block, preferred_element_type=jnp.float32
        )
        grad_k = grad_k + jnp.einsum(
            "jhe,hde->jhd", values_in.astype(jnp.float32) * key_decay, back, precision=highest
        )
        grad_v = jnp.einsum("hij,ihe->jhe", weights, dout, preferred_element_type=jnp.float32)
        grad_v = grad_v + jnp.einsum(
            "jhd,hde->jhe", keys_in.astype(jnp.float32) * key_decay, back, precision=highest
        )
        grad_q_parts.insert(0, grad_q.astype(jnp.bfloat16))
        grad_k_parts.insert(0, grad_k.astype(jnp.bfloat16))
        grad_v_parts.insert(0, grad_v.astype(jnp.bfloat16))
        back = block_decay * back + query_terms[number]
    flat_width = head_count * head_width
    grad_query = grad_q_parts[0].reshape(row_count, flat_width)
    grad_key = grad_k_parts[0].reshape(row_count, flat_width)
    grad_value = grad_v_parts[0].reshape(row_count, flat_width)
    return (grad_query, grad_key, grad_value)


def solution(mesh):
    return jax.shard_map(
        body,
        mesh=mesh,
        in_specs=(
            P("ctx", "head"),
            P("ctx", "head"),
            P("ctx", "head"),
            P("head", None),
            P(("ctx", "head"), None),
            P("head"),
        ),
        out_specs=(P("ctx", "head"), P("ctx", "head"), P("ctx", "head")),
        check_vma=False,
    )
```

profile of v0, /device:TPU:8, one launch (start us, length us, event | category | flops | bytes accessed | tf_op | source)
XLA Modules:
  0.0 561.5 jit_solution(6718802182635984117)
XLA Ops:
  7.9 1.1 copy.51
  9.0 1.1 copy.54
  11.9 1.4 dynamic-slice
  14.1 156.6 %all-reduce = f32[192]{0:T(256)S(1)} all-reduce(f32[192]{0:T(256)S(1)} %fusion.21), channel_id=2, replica_groups=mesh['ctx'=64,'head'=16] {'ctx'}, use_global_device_ids=true, to_apply=%add | all-reduce | flops 192 | bytes 1536
  170.9 1.1 copy.50
  172.5 5.2 fusion.5
  177.9 70.0 %all-gather.9.cloned.1.call-done = f32[192,128,128]{2,1,0:T(8,128)} async-done(((f32[3,128,128]{2,1,0:T(8,128)}), f32[192,128,128]{2,1,0:T(8,128)}) %all-gather.9.cloned.1.call-update) | async-done | bytes 12582928 | tf_op jit(solution)/shard_map/all_gather | solution.py:16
  252.4 232.3 %all-gather.11.cloned.1.call-done = f32[192,128,128]{2,1,0:T(8,128)} async-done(((f32[3,128,128]{2,1,0:T(8,128)}), f32[192,128,128]{2,1,0:T(8,128)}) %all-gather.11.cloned.1.call-update) | async-done | bytes 12582928 | tf_op jit(solution)/shard_map/all_gather | solution.py:16
  484.8 67.6 %while.27 = (s32[]{:T(128)}, f32[3,128,128]{2,1,0:T(8,128)S(1)}, s32[]{:T(128)}, f32[64,3]{1,0:T(8,128)S(1)}, f32[64,3,128,128]{3,2,1,0:T(8,128)}, /*index=5*/s32[]{:T(128)}, s32[]{:T(128)}, s32[]{:T(128)}, s32[]{:T(128)}) while((s32[]{:T(128)}, f32[3,128,128]{2,1,0:T(8,128)S(1)}, s32[]{:T(128)}, f32[64,3]{1,0:T(8,128)S(1)}, ...), condition=%wide.region_5.6_spmd, body=%wide.region_4.5_spmd.sunk | while | flops 98310 | bytes 590015 | solution.py:25
  486.9 1.0 bitcast_add_fusion.5
  489.1 1.0 bitcast_add_fusion.5
  492.3 1.0 bitcast_add_fusion.5
  494.5 1.0 bitcast_add_fusion.5
  496.6 1.0 bitcast_add_fusion.5
  499.8 1.0 bitcast_add_fusion.5
  502.0 1.0 bitcast_add_fusion.5
  507.3 1.0 bitcast_add_fusion.5
  509.5 1.0 bitcast_add_fusion.5
  512.7 1.0 bitcast_add_fusion.5
  514.8 1.0 bitcast_add_fusion.5
  517.0 1.0 bitcast_add_fusion.5
  520.2 1.0 bitcast_add_fusion.5
  522.3 1.0 bitcast_add_fusion.5
  527.7 1.0 bitcast_add_fusion.5
  529.9 1.0 bitcast_add_fusion.5
  533.1 1.0 bitcast_add_fusion.5
  535.2 1.0 bitcast_add_fusion.5
  537.4 1.0 bitcast_add_fusion.5
  540.6 1.0 bitcast_add_fusion.5
  542.7 1.0 bitcast_add_fusion.5
  548.1 1.0 bitcast_add_fusion.5
  550.2 1.0 bitcast_add_fusion.5
  (142 shorter events, 52.6 us)
Async XLA Ops:
  7.2 165.4 %all-gather.7.cloned.1.call-start = ((), (), s32[]{:S(2)}) async-start(), calls=%async_computation | async-start | bytes 3342336 | tf_op jit(solution)/shard_map/all_gather | solution.py:38
  7.9 240.0 %all-gather.9.cloned.1.call-start = ((), (), s32[]{:S(2)}) async-start(), calls=%async_computation.1 | async-start | bytes 12779520 | tf_op jit(solution)/shard_map/all_gather | solution.py:16
  11.9 472.9 %all-gather.11.cloned.1.call-start = ((), (), s32[]{:S(2)}) async-start(), calls=%async_computation.2 | async-start | bytes 12779520 | tf_op jit(solution)/shard_map/all_gather | solution.py:16
Sparse Core Ops, SparseCore 0:
  10.7 55.7 all-gather.6
  71.2 176.6 all-gather.8
  252.6 232.1 all-gather.10
where the time goes:
time: 563 us; the launch traced here: 562 us
  waiting for transfers between devices  303 us (54%)
  blocking collectives  157 us (28%)
  other arithmetic  66.1 us (12%)
  between operations  14.6 us (3%)
  matrix products  11 us (2%)
  local copies, waits for them, and re-layouts  8.08 us (1%)
    all_gather x2, waiting for transfers between devices, prefix(): gathered = jax.tree.map(lambda a: lax.all_gather(a, axis), part)  302 us
    unnamed x1, blocking collectives  157 us
    add x63, other arithmetic, combine(): later[0][:, None, None] * earlier[1] + later[1]  64.8 us
  transfers between devices with their start and end apart: 3, of which 2 were waited for; matrix products, arithmetic and copies ran while one was open for 3% of the time, Pallas kernels for 0%

commit v1 on v0

v1 whole, which is shorter than its diff:
```python
import functools

import jax
import jax.numpy as jnp
from jax import lax
from jax.experimental import pallas as pl
from jax.experimental.pallas import tpu as pltpu
from jax.sharding import PartitionSpec as P

MESH = pl.DeviceIdType.MESH
GROUP = 8
CHUNKS = 4
EPSILON = 1e-06
F32 = jnp.float32
BF16 = jnp.bfloat16
NN = (((1,), (0,)), ((), ()))
NT = (((1,), (1,)), ((), ()))
TN = (((0,), (0,)), ((), ()))


def dot(a, b, dims):
    return lax.dot_general(a, b, dims, preferred_element_type=F32)


def kernel(
    n_ctx,
    n_head,
    lr_ref,
    q_hbm,
    k_hbm,
    v_hbm,
    w_hbm,
    g_hbm,
    gq_ref,
    gk_ref,
    gv_ref,
    q,
    k,
    v,
    w,
    g,
    dn,
    scores,
    att,
    inv,
    dout,
    a_send,
    a_recv,
    pre,
    b_send,
    b_recv,
    carry,
    c_send,
    state,
    load_sem,
    ring_ssem,
    ring_rsem,
    pair_ssem,
    pair_rsem,
    a_ssem,
    a_rsem,
    b_ssem,
    b_rsem,
    c_ssem,
    c_rsem,
):
    rows, width = q.shape
    heads = width // 128
    shard_rows = rows // n_head
    chunk = g.shape[2] // CHUNKS
    piece = 128 // GROUP
    ny, n_hi = n_head // 2, n_ctx // GROUP
    half = ny // 2
    ctx, head = lax.axis_index("ctx"), lax.axis_index("head")
    y, core = head // 2, head % 2
    hi, lo = ctx // GROUP, ctx % GROUP

    loads = [
        pltpu.make_async_copy(src, dst, load_sem.at[i])
        for i, (src, dst) in enumerate(
            ((k_hbm, k), (v_hbm, v), (q_hbm, q), (g_hbm, g.at[head]), (w_hbm, w))
        )
    ]
    for load in loads:
        load.start()

    other = y * 2 + 1 - core
    partners = [(ctx, ((y + step) % ny) * 2 + core) for step in (1, ny - 1)] + [(ctx, other)]
    partners += [(hi * GROUP + (lo + step) % GROUP, head) for step in range(1, GROUP)]
    partners += [(((hi + step) % n_hi) * GROUP + lo, head) for step in range(1, n_hi)]
    barrier = pltpu.get_barrier_semaphore()
    for partner in partners:
        pl.semaphore_signal(barrier, inc=1, device_id=partner, device_id_type=MESH)
    pl.semaphore_wait(barrier, len(partners))

    def push(src, dst, ssem, rsem, device):
        return pltpu.make_async_remote_copy(
            src_ref=src,
            dst_ref=dst,
            send_sem=ssem,
            recv_sem=rsem,
            device_id=device,
            device_id_type=MESH,
        )

    def place(d, s, c):
        return ((y + (ny - s if d == 0 else s)) % ny) * 2 + c

    def carried(d, s, c):
        return s < half or (c < CHUNKS // 2) == (d == 0)

    def cols(c):
        return pl.ds(c * chunk, chunk)

    def ring(d, s, c):
        block = g.at[place(d, s, core), :, cols(c)]
        src = g_hbm.at[:, cols(c)] if s == 0 else block
        return push(
            src, block, ring_ssem.at[d, s, c], ring_rsem.at[d, s, c], (ctx, place(1 - d, 1, core))
        )

    def ring_in(d, s, c):
        block = g.at[place(d, s, core), :, cols(c)]
        return push(
            block, block, ring_ssem.at[d, s - 1, c], ring_rsem.at[d, s - 1, c], (ctx, other)
        )

    def pair(d, s, c):
        block = g.at[place(d, s, core), :, cols(c)]
        src = g_hbm.at[:, cols(c)] if s == 0 else block
        return push(src, block, pair_ssem.at[d, s, c], pair_rsem.at[d, s, c], (ctx, other))

    def pair_in(d, s, c):
        block = g.at[place(d, s, 1 - core), :, cols(c)]
        return push(block, block, pair_ssem.at[d, s, c], pair_rsem.at[d, s, c], (ctx, other))

    sent = []

    def start(copy):
        copy.start()
        sent.append(copy)

    for c in range(CHUNKS):
        for d in range(2):
            start(ring(d, 0, c))
    for c in range(CHUNKS):
        start(pair(0, 0, c))

    def ring_step(s):
        for c in range(CHUNKS):
            for d in range(2):
                if carried(d, s, c):
                    ring_in(d, s, c).wait_recv()
                    if s < half and carried(d, s + 1, c):
                        start(ring(d, s, c))
                    start(pair(d, s, c))

    def pair_step(s):
        for c in range(CHUNKS):
            for d in range(2):
                if carried(d, s, c) and (s > 0 or d == 0):
                    pair_in(d, s, c).wait_recv()

    def project(steps):
        blocks = []
        for s in steps:
            for d in range(2):
                if (s > 0 or d == 0) and (s < half or d == 0):
                    blocks += [place(d, s, core), place(d, s, 1 - core)]
        a = jnp.concatenate([g[block] for block in blocks], axis=0)
        out = dot(a, w[...], NT).astype(BF16)
        for i, block in enumerate(blocks):
            at = pl.ds(pl.multiple_of(block * shard_rows, shard_rows), shard_rows)
            dn[at, :] = out[i * shard_rows : (i + 1) * shard_rows]

    rates = [lr_ref[h] for h in range(heads)]
    lanes = jnp.concatenate([jnp.full((1, 128), rate, F32) for rate in rates], axis=1)
    offset = lax.broadcasted_iota(jnp.int32, (rows, 128), 0).astype(F32)

    def query_decay(h):
        return jnp.exp((offset + 1.0) * rates[h])

    def key_decay(h):
        return jnp.exp((rows - 1.0 - offset) * rates[h])

    def decay_mask(h):
        spread = lax.broadcasted_iota(jnp.int32, (rows, rows), 0) - lax.broadcasted_iota(
            jnp.int32, (rows, rows), 1
        )
        powers = jnp.exp(jnp.maximum(spread, 0).astype(F32) * rates[h])
        return jnp.where(spread >= 0, powers, 0.0)

    def device_decay(power):
        return jnp.exp((power * rows * 1.0) * lanes)

    def of(h):
        return slice(h * 128, (h + 1) * 128)

    def strip(place_of):
        return pl.ds(pl.multiple_of(place_of * piece, piece), piece)

    def peer(step):
        return (lo + step) % GROUP

    def a_start(t):
        for s in range(1, GROUP):
            start(
                push(
                    a_send.at[t, strip(peer(s))],
                    a_recv.at[t, lo],
                    a_ssem.at[t, s - 1],
                    a_rsem.at[t, s - 1],
                    (hi * GROUP + peer(s), head),
                )
            )
        a_recv[t, lo] = a_send[t, strip(lo)]

    def b_copy(t, s, target):
        return push(
            b_send.at[t],
            b_recv.at[t, s - 1],
            b_ssem.at[t, s - 1],
            b_rsem.at[t, s - 1],
            (target * GROUP + lo, head),
        )

    def a_finish(t):
        for s in range(1, GROUP):
            block = a_recv.at[t, peer(GROUP - s)]
            push(block, block, a_ssem.at[t, s - 1], a_rsem.at[t, s - 1], (ctx, other)).wait_recv()
        step = device_decay(1)
        total = jnp.zeros((piece, width), F32)
        for i in range(GROUP) if t == 0 else reversed(range(GROUP)):
            pre[t, i] = total
            total = step * total + a_recv[t, i].astype(F32)
        b_send[t] = total.astype(BF16)
        for s in range(1, n_hi):
            target = hi + s if t == 0 else hi - s

            @pl.when((target < n_hi) & (target >= 0))
            def _():
                b_copy(t, s, target).start()

    def b_finish(t):
        carry[...] = jnp.zeros_like(carry)
        for s in range(1, n_hi):
            source = hi - s if t == 0 else hi + s

            @pl.when((source < n_hi) & (source >= 0))
            def _():
                b_copy(t, s, hi).wait_recv()
                carry[...] += device_decay((s - 1) * GROUP) * b_recv[t, s - 1].astype(F32)

        for i in range(GROUP):
            power = i if t == 0 else GROUP - 1 - i
            c_send[t, i] = (pre[t, i] + device_decay(power) * carry[...]).astype(BF16)
        for s in range(1, GROUP):
            start(
                push(
                    c_send.at[t, peer(s)],
                    state.at[t, strip(lo)],
                    c_ssem.at[t, s - 1],
                    c_rsem.at[t, s - 1],
                    (hi * GROUP + peer(s), head),
                )
            )
        state[t, strip(lo), :] = c_send[t, lo]

    def b_drain(t):
        for s in range(1, n_hi):
            target = hi + s if t == 0 else hi - s

            @pl.when((target < n_hi) & (target >= 0))
            def _():
                b_copy(t, s, target).wait_send()

    def c_finish(t):
        for s in range(1, GROUP):
            block = state.at[t, strip(peer(GROUP - s))]
            push(block, block, c_ssem.at[t, s - 1], c_rsem.at[t, s - 1], (ctx, other)).wait_recv()

    loads[0].wait()
    loads[1].wait()
    for h in range(heads):
        decayed = (k[:, of(h)].astype(F32) * key_decay(h)).astype(BF16)
        a_send[0, :, of(h)] = dot(decayed, v[:, of(h)], TN).astype(BF16)
    a_start(0)
    loads[2].wait()
    ring_step(1)
    a_finish(0)
    for h in range(heads):
        product = dot(q[:, of(h)], k[:, of(h)], NT)
        weights = (product * decay_mask(h)).astype(BF16)
        scores[h] = weights
        att[:, of(h)] = dot(weights, v[:, of(h)], NN)
    for s in range(2, half):
        ring_step(s)
        if s == 2:
            b_finish(0)
    if half <= 2:
        b_finish(0)
    loads[3].wait()
    loads[4].wait()
    early = range(0, half - 1)
    for s in early:
        pair_step(s)
    project(early)
    c_finish(0)
    for h in range(heads):
        attended = att[:, of(h)] + query_decay(h) * dot(q[:, of(h)], state[0, :, of(h)], NN)
        inverse = lax.rsqrt(jnp.mean(attended * attended, axis=-1, keepdims=True) + EPSILON)
        att[:, of(h)] = attended * inverse
        inv[:, of(h)] = jnp.broadcast_to(inverse, (rows, 128))
    ring_step(half)
    pair_step(half - 1)
    pair_step(half)
    project(range(half - 1, half + 1))

    for h in range(heads):
        cot, normed = dn[:, of(h)].astype(F32), att[:, of(h)]
        along = jnp.mean(cot * normed, axis=-1, keepdims=True)
        grad = ((cot - normed * along) * inv[:, of(h)]).astype(BF16)
        dout[:, of(h)] = grad
        decayed = (q[:, of(h)].astype(F32) * query_decay(h)).astype(BF16)
        a_send[1, :, of(h)] = dot(decayed, grad, TN).astype(BF16)
    a_start(1)
    for h in range(heads):
        product = dot(dout[:, of(h)], v[:, of(h)], NT)
        dweights = (product * decay_mask(h)).astype(BF16)
        grad_q = dot(dweights, k[:, of(h)], NN)
        grad_q += query_decay(h) * dot(dout[:, of(h)], state[0, :, of(h)], NT)
        gq_ref[:, of(h)] = grad_q.astype(BF16)
        att[:, of(h)] = dot(dweights, q[:, of(h)], TN)
    a_finish(1)
    for h in range(heads):
        inv[:, of(h)] = dot(scores[h], dout[:, of(h)], TN)
    b_finish(1)
    c_finish(1)
    for h in range(heads):
        back = state[1, :, of(h)]
        decay = key_decay(h)
        gk_ref[:, of(h)] = (att[:, of(h)] + decay * dot(v[:, of(h)], back, NT)).astype(BF16)
        gv_ref[:, of(h)] = (inv[:, of(h)] + decay * dot(k[:, of(h)], back, NN)).astype(BF16)
    for copy in sent:
        copy.wait_send()
    b_drain(0)
    b_drain(1)


def body(n_ctx, n_head, query, key_in, value, out_weight, grad_layer, decay_exp):
    log_rate = jnp.log1p(-jnp.exp2(-decay_exp.astype(F32)))
    rows, width = query.shape
    model = grad_layer.shape[1]
    heads = decay_exp.shape[0]
    shard_rows = grad_layer.shape[0]
    half = n_head // 4
    piece = 128 // GROUP
    n_hi = n_ctx // GROUP
    vmem = pl.BlockSpec(memory_space=pltpu.VMEM)
    hbm = pl.BlockSpec(memory_space=pl.ANY)
    dma = pltpu.SemaphoreType.DMA
    out = jax.ShapeDtypeStruct((rows, width), BF16)
    return pl.pallas_call(
        functools.partial(kernel, n_ctx, n_head),
        out_shape=(out, out, out),
        in_specs=[pl.BlockSpec(memory_space=pltpu.SMEM)] + [hbm] * 5,
        out_specs=(vmem, vmem, vmem),
        scratch_shapes=[
            pltpu.VMEM((rows, width), BF16),
            pltpu.VMEM((rows, width), BF16),
            pltpu.VMEM((rows, width), BF16),
            pltpu.VMEM((width, model), BF16),
            pltpu.VMEM((n_head, shard_rows, model), BF16),
            pltpu.VMEM((rows, width), BF16),
            pltpu.VMEM((heads, rows, rows), BF16),
            pltpu.VMEM((rows, width), F32),
            pltpu.VMEM((rows, width), F32),
            pltpu.VMEM((rows, width), BF16),
            pltpu.VMEM((2, 128, width), BF16),
            pltpu.VMEM((2, GROUP, piece, width), BF16),
            pltpu.VMEM((2, GROUP, piece, width), F32),
            pltpu.VMEM((2, piece, width), BF16),
            pltpu.VMEM((2, max(n_hi - 1, 1), piece, width), BF16),
            pltpu.VMEM((piece, width), F32),
            pltpu.VMEM((2, GROUP, piece, width), BF16),
            pltpu.VMEM((2, 128, width), BF16),
            dma((5,)),
            dma((2, half, CHUNKS)),
            dma((2, half, CHUNKS)),
            dma((2, half + 1, CHUNKS)),
            dma((2, half + 1, CHUNKS)),
            dma((2, GROUP - 1)),
            dma((2, GROUP - 1)),
            dma((2, max(n_hi - 1, 1))),
            dma((2, max(n_hi - 1, 1))),
            dma((2, GROUP - 1)),
            dma((2, GROUP - 1)),
        ],
        compiler_params=pltpu.CompilerParams(collective_id=0, has_side_effects=True),
    )(log_rate, query, key_in, value, out_weight, grad_layer)


def solution(mesh):
    return jax.shard_map(
        functools.partial(body, mesh.shape["ctx"], mesh.shape["head"]),
        mesh=mesh,
        in_specs=(
            P("ctx", "head"),
            P("ctx", "head"),
            P("ctx", "head"),
            P("head", None),
            P(("ctx", "head"), None),
            P("head"),
        ),
        out_specs=(P("ctx", "head"), P("ctx", "head"), P("ctx", "head")),
        check_vma=False,
    )
```

time: 563 us -> 72.7 us (0.13)
  the two profiles are of different devices: /device:TPU:8 before, /device:TPU:2 now
where the time goes in v1:
time: 72.7 us; the launch traced here: 72.5 us
  Pallas kernels  65.8 us (91%)
  local copies, waits for them, and re-layouts  4.87 us (7%)
  other arithmetic  1.19 us (2%)
    pallas_call x1, Pallas kernels, body(): pl.pallas_call(functools.partial(kernel, n_ctx, n_head), out_shape=(out,...  65.8 us
    unnamed x3, local copies, waits for them, and re-layouts  4.87 us

profile of v1, /device:TPU:2, one launch (start us, length us, event | category | flops | bytes accessed | tf_op | source)
XLA Modules:
  0.0 72.5 jit_solution(9555601661494711401)
XLA Ops:
  0.6 1.2 %negate_log-plus-one_fusion.lr_ref = f32[3]{0:T(128)} fusion(s32[3]{0:T(128)} %param.11), kind=kLoop, calls=%fused_computation | loop fusion | flops 12 | bytes 24 | tf_op jit(solution)/shard_map/log1p | solution.py:351
  1.8 65.8 %shard_map.85 = (bf16[256,384]{1,0:T(8,128)(2,1)}, bf16[256,384]{1,0:T(8,128)(2,1)}, bf16[256,384]{1,0:T(8,128)(2,1)}) custom-call(f32[3]{0:T(128)} %negate_log-plus-one_fusion.lr_ref, bf16[256,384]{1,0:T(8,128)(2,1)} %q_hbm.1, bf16[256,384]{1,0:T(8,128)(2,1)} %k_hbm.1, bf16[256,384]{1,0:T(8,128)(2,1)} %v_hbm.1, bf16[384,6144]{1,0:T(8,128)(2,1)} %w_hbm.1, ...), custom_call_target="tpu_custom_call" | custom-call | tf_op jit(solution)/shard_map/pallas_call | solution.py:363
  67.6 1.6 %copy.12 = bf16[256,384]{1,0:T(8,128)(2,1)} copy(bf16[256,384]{1,0:T(8,128)(2,1)} %get-tuple-element.6) | data formatting | bytes 393216
  69.2 1.6 %copy.13 = bf16[256,384]{1,0:T(8,128)(2,1)} copy(bf16[256,384]{1,0:T(8,128)(2,1)} %get-tuple-element.7) | data formatting | bytes 393216
  70.9 1.6 %copy.14 = bf16[256,384]{1,0:T(8,128)(2,1)} copy(bf16[256,384]{1,0:T(8,128)(2,1)} %get-tuple-element.8) | data formatting | bytes 393216

commit v2 on v1

--- a/solution.py
+++ b/solution.py
@@ -25,7 +25,7 @@
 def kernel(
     n_ctx,
     n_head,
-    lr_ref,
+    decay_ref,
     q_hbm,
     k_hbm,
     v_hbm,
@@ -50,6 +50,7 @@
     b_send,
     b_recv,
     carry,
+    part,
     c_send,
     state,
     load_sem,
@@ -63,6 +64,7 @@
     b_rsem,
     c_ssem,
     c_rsem,
+    ready,
 ):
     rows, width = q.shape
     heads = width // 128
@@ -85,13 +87,29 @@
         load.start()
 
     other = y * 2 + 1 - core
-    partners = [(ctx, ((y + step) % ny) * 2 + core) for step in (1, ny - 1)] + [(ctx, other)]
-    partners += [(hi * GROUP + (lo + step) % GROUP, head) for step in range(1, GROUP)]
-    partners += [(((hi + step) % n_hi) * GROUP + lo, head) for step in range(1, n_hi)]
+    near = [(ctx, ((y + step) % ny) * 2 + core) for step in (1, ny - 1)] + [(ctx, other)]
+    near += [(hi * GROUP + (lo + step) % GROUP, head) for step in range(1, GROUP)]
     barrier = pltpu.get_barrier_semaphore()
-    for partner in partners:
+    for partner in near:
         pl.semaphore_signal(barrier, inc=1, device_id=partner, device_id_type=MESH)
-    pl.semaphore_wait(barrier, len(partners))
+    for s in range(1, n_hi):
+
+        @pl.when(hi + s < n_hi)
+        def _():
+            later = ((hi + s) * GROUP + lo, head)
+            pl.semaphore_signal(barrier, inc=1, device_id=later, device_id_type=MESH)
+
+    pl.semaphore_wait(barrier, len(near) + hi)
+
+    def greet():
+        for s in range(1, n_hi):
+
+            @pl.when(hi - s >= 0)
+            def _():
+                earlier = ((hi - s) * GROUP + lo, head)
+                pl.semaphore_signal(
+                    ready.at[s - 1], inc=1, device_id=earlier, device_id_type=MESH
+                )
 
     def push(src, dst, ssem, rsem, device):
         return pltpu.make_async_remote_copy(
@@ -146,42 +164,57 @@
     for c in range(CHUNKS):
         start(pair(0, 0, c))
 
-    def ring_step(s):
-        for c in range(CHUNKS):
-            for d in range(2):
-                if carried(d, s, c):
-                    ring_in(d, s, c).wait_recv()
-                    if s < half and carried(d, s + 1, c):
-                        start(ring(d, s, c))
-                    start(pair(d, s, c))
-
-    def pair_step(s):
-        for c in range(CHUNKS):
-            for d in range(2):
-                if carried(d, s, c) and (s > 0 or d == 0):
-                    pair_in(d, s, c).wait_recv()
-
-    def project(steps):
+    greet()
+
+    def ring_chunk(s, c):
+        for d in range(2):
+            if carried(d, s, c):
+                ring_in(d, s, c).wait_recv()
+                if s < half and carried(d, s + 1, c):
+                    start(ring(d, s, c))
+                start(pair(d, s, c))
+
+    def pair_chunk(s, c):
+        for d in range(2):
+            if carried(d, s, c) and (s > 0 or d == 0):
+                pair_in(d, s, c).wait_recv()
+
+    def blocks_of(steps):
         blocks = []
         for s in steps:
             for d in range(2):
                 if (s > 0 or d == 0) and (s < half or d == 0):
                     blocks += [place(d, s, core), place(d, s, 1 - core)]
-        a = jnp.concatenate([g[block] for block in blocks], axis=0)
-        out = dot(a, w[...], NT).astype(BF16)
-        for i, block in enumerate(blocks):
+        return blocks
+
+    def project(steps, c, first):
+        blocks = blocks_of(steps)
+        a = jnp.concatenate([g[block, :, cols(c)] for block in blocks], axis=0)
+        out = dot(a, w[:, cols(c)], NT)
+        at = slice(0, len(blocks) * shard_rows)
+        part[at, :] = out if first else part[at, :] + out
+
+    def place_rows(steps):
+        for i, block in enumerate(blocks_of(steps)):
             at = pl.ds(pl.multiple_of(block * shard_rows, shard_rows), shard_rows)
-            dn[at, :] = out[i * shard_rows : (i + 1) * shard_rows]
-
-    rates = [lr_ref[h] for h in range(heads)]
-    lanes = jnp.concatenate([jnp.full((1, 128), rate, F32) for rate in rates], axis=1)
+            dn[at, :] = part[i * shard_rows : (i + 1) * shard_rows, :].astype(BF16)
+
+    def rate_of(h):
+        u = jnp.exp2(jnp.full((1, rows), -decay_ref[h].astype(F32)))
+        tail = jnp.full_like(u, 1.0 / 9)
+        for n in range(8, 0, -1):
+            tail = 1.0 / n + u * tail
+        return -u * tail
+
+    rates = [rate_of(h) for h in range(heads)]
+    lanes = jnp.concatenate([rate[:, :128] for rate in rates], axis=1)
     offset = lax.broadcasted_iota(jnp.int32, (rows, 128), 0).astype(F32)
 
     def query_decay(h):
-        return jnp.exp((offset + 1.0) * rates[h])
+        return jnp.exp((offset + 1.0) * rates[h][:, :128])
 
     def key_decay(h):
-        return jnp.exp((rows - 1.0 - offset) * rates[h])
+        return jnp.exp((rows - 1.0 - offset) * rates[h][:, :128])
 
     def decay_mask(h):
         spread = lax.broadcasted_iota(jnp.int32, (rows, rows), 0) - lax.broadcasted_iota(
@@ -234,11 +267,15 @@
             pre[t, i] = total
             total = step * total + a_recv[t, i].astype(F32)
         b_send[t] = total.astype(BF16)
-        for s in range(1, n_hi):
+
+    def b_start(t, steps):
+        for s in steps:
             target = hi + s if t == 0 else hi - s
 
             @pl.when((target < n_hi) & (target >= 0))
             def _():
+                if t == 0:
+                    pl.semaphore_wait(ready.at[s - 1], 1)
                 b_copy(t, s, target).start()
 
     def b_finish(t):
@@ -286,35 +323,43 @@
         a_send[0, :, of(h)] = dot(decayed, v[:, of(h)], TN).astype(BF16)
     a_start(0)
     loads[2].wait()
-    ring_step(1)
-    a_finish(0)
     for h in range(heads):
         product = dot(q[:, of(h)], k[:, of(h)], NT)
         weights = (product * decay_mask(h)).astype(BF16)
         scores[h] = weights
         att[:, of(h)] = dot(weights, v[:, of(h)], NN)
-    for s in range(2, half):
-        ring_step(s)
-        if s == 2:
-            b_finish(0)
-    if half <= 2:
-        b_finish(0)
     loads[3].wait()
     loads[4].wait()
-    early = range(0, half - 1)
-    for s in early:
-        pair_step(s)
-    project(early)
+    early, late = range(0, half - 1), range(half - 1, half + 1)
+    for s in range(1, half):
+        for c in range(CHUNKS):
+            ring_chunk(s, c)
+            if (s, c) == (1, CHUNKS - 2):
+                a_finish(0)
+                b_start(0, range(1, min(3, n_hi)))
+            if (s, c) == (2, 1) or (half == 2 and c == CHUNKS - 1):
+                b_start(0, range(3, n_hi))
+                b_finish(0)
+            if s == half - 1:
+                for earlier in early:
+                    pair_chunk(earlier, c)
+                project(early, c, c == 0)
+    place_rows(early)
     c_finish(0)
-    for h in range(heads):
-        attended = att[:, of(h)] + query_decay(h) * dot(q[:, of(h)], state[0, :, of(h)], NN)
-        inverse = lax.rsqrt(jnp.mean(attended * attended, axis=-1, keepdims=True) + EPSILON)
-        att[:, of(h)] = attended * inverse
-        inv[:, of(h)] = jnp.broadcast_to(inverse, (rows, 128))
-    ring_step(half)
-    pair_step(half - 1)
-    pair_step(half)
-    project(range(half - 1, half + 1))
+    order = [c for pairs in zip(range(CHUNKS // 2), range(CHUNKS // 2, CHUNKS)) for c in pairs]
+    for c in order:
+        ring_chunk(half, c)
+        if c == CHUNKS // 2:
+            for h in range(heads):
+                attended = att[:, of(h)] + query_decay(h) * dot(q[:, of(h)], state[0, :, of(h)], NN)
+                inverse = lax.rsqrt(jnp.mean(attended * attended, axis=-1, keepdims=True) + EPSILON)
+                att[:, of(h)] = attended * inverse
+                inv[:, of(h)] = jnp.broadcast_to(inverse, (rows, 128))
+    for c in order:
+        for s in late:
+            pair_chunk(s, c)
+        project(late, c, c == 0)
+    place_rows(late)
 
     for h in range(heads):
         cot, normed = dn[:, of(h)].astype(F32), att[:, of(h)]
@@ -332,6 +377,7 @@
         gq_ref[:, of(h)] = grad_q.astype(BF16)
         att[:, of(h)] = dot(dweights, q[:, of(h)], TN)
     a_finish(1)
+    b_start(1, range(1, n_hi))
     for h in range(heads):
         inv[:, of(h)] = dot(scores[h], dout[:, of(h)], TN)
     b_finish(1)
@@ -347,8 +393,18 @@
     b_drain(1)
 
 
+def store_kernel(gq_ref, gk_ref, gv_ref, gq_hbm, gk_hbm, gv_hbm, sem):
+    copies = [
+        pltpu.make_async_copy(src, dst, sem.at[i])
+        for i, (src, dst) in enumerate(((gq_ref, gq_hbm), (gk_ref, gk_hbm), (gv_ref, gv_hbm)))
+    ]
+    for copy in copies:
+        copy.start()
+    for copy in copies:
+        copy.wait()
+
+
 def body(n_ctx, n_head, query, key_in, value, out_weight, grad_layer, decay_exp):
-    log_rate = jnp.log1p(-jnp.exp2(-decay_exp.astype(F32)))
     rows, width = query.shape
     model = grad_layer.shape[1]
     heads = decay_exp.shape[0]
@@ -357,10 +413,10 @@
     piece = 128 // GROUP
     n_hi = n_ctx // GROUP
     vmem = pl.BlockSpec(memory_space=pltpu.VMEM)
-    hbm = pl.BlockSpec(memory_space=pl.ANY)
+    hbm = pl.BlockSpec(memory_space=pltpu.HBM)
     dma = pltpu.SemaphoreType.DMA
-    out = jax.ShapeDtypeStruct((rows, width), BF16)
-    return pl.pallas_call(
+    out = pltpu.VMEM((rows, width), BF16)
+    grads = pl.pallas_call(
         functools.partial(kernel, n_ctx, n_head),
         out_shape=(out, out, out),
         in_specs=[pl.BlockSpec(memory_space=pltpu.SMEM)] + [hbm] * 5,
@@ -382,6 +438,7 @@
             pltpu.VMEM((2, piece, width), BF16),
             pltpu.VMEM((2, max(n_hi - 1, 1), piece, width), BF16),
             pltpu.VMEM((piece, width), F32),
+            pltpu.VMEM((rows, width), F32),
             pltpu.VMEM((2, GROUP, piece, width), BF16),
             pltpu.VMEM((2, 128, width), BF16),
             dma((5,)),
@@ -395,9 +452,20 @@
             dma((2, max(n_hi - 1, 1))),
             dma((2, GROUP - 1)),
             dma((2, GROUP - 1)),
+            pltpu.SemaphoreType.REGULAR((max(n_hi - 1, 1),)),
         ],
-        compiler_params=pltpu.CompilerParams(collective_id=0, has_side_effects=True),
-    )(log_rate, query, key_in, value, out_weight, grad_layer)
+        compiler_params=pltpu.CompilerParams(
+            collective_id=0, has_side_effects=True, vmem_limit_bytes=66 * 10**6
+        ),
+    )(decay_exp, query, key_in, value, out_weight, grad_layer)
+    return pl.pallas_call(
+        store_kernel,
+        out_shape=(jax.ShapeDtypeStruct((rows, width), BF16),) * 3,
+        in_specs=[vmem] * 3,
+        out_specs=[hbm] * 3,
+        scratch_shapes=[dma((3,))],
+        compiler_params=pltpu.CompilerParams(vmem_limit_bytes=4 * 2**20),
+    )(*grads)
 
 
 def solution(mesh):

time: 72.7 us -> 63.5 us (0.87)
  the two profiles are of different devices: /device:TPU:2 before, /device:TPU:8 now
where the time goes in v2:
time: 63.5 us; the launch traced here: 63 us
  Pallas kernels  62.3 us (98%)
  between operations  0.64 us (1%)
    pallas_call x1, Pallas kernels, body(): pl.pallas_call(functools.partial(kernel, n_ctx, n_head), out_shape=(out,...  61.5 us

profile of v2, /device:TPU:8, one launch (start us, length us, event | category | flops | bytes accessed | tf_op | source)
XLA Modules:
  0.0 63.0 jit_solution(7689484616395015704)
XLA Ops:
  0.6 61.5 %shard_map.85 = (bf16[256,384]{1,0:T(8,128)(2,1)S(1)}, bf16[256,384]{1,0:T(8,128)(2,1)S(1)}, bf16[256,384]{1,0:T(8,128)(2,1)S(1)}) custom-call(s32[3]{0:T(128)} %decay_ref.1, bf16[256,384]{1,0:T(8,128)(2,1)} %q_hbm.1, bf16[256,384]{1,0:T(8,128)(2,1)} %k_hbm.1, bf16[256,384]{1,0:T(8,128)(2,1)} %v_hbm.1, bf16[384,6144]{1,0:T(8,128)(2,1)} %w_hbm.1, ...), custom_call_target="tpu_custom_call" | custom-call | tf_op jit(solution)/shard_map/pallas_call | solution.py:419
  62.1 0.8 %shard_map.86 = (bf16[256,384]{1,0:T(8,128)(2,1)}, bf16[256,384]{1,0:T(8,128)(2,1)}, bf16[256,384]{1,0:T(8,128)(2,1)}) custom-call(bf16[256,384]{1,0:T(8,128)(2,1)S(1)} %get-tuple-element.6.gq_ref, bf16[256,384]{1,0:T(8,128)(2,1)S(1)} %get-tuple-element.7.gk_ref, bf16[256,384]{1,0:T(8,128)(2,1)S(1)} %get-tuple-element.8.gv_ref), custom_call_target="tpu_custom_call" | custom-call | tf_op jit(solution)/shard_map/pallas_call | solution.py:461
